TPU v7x, 32 devices: a whole 2x2x4 slice. The times are simulated.
32 devices in a mesh: node: 4 (over y, x), feat: 4 (over z), tm: 2 (over core).
Axes of the slice: x: 2, y: 2, z: 4, core: 2. Of those that a mesh axis runs over, the one named last changes fastest.
Arguments:
- tensor: float32 [2, 16384, 4096], P('tm', 'node', 'feat'), may hold values from -6 to 6
- basis: float32 [16384, 128], P('node'), may hold values from -0.046875 to 0.046875
Outputs:
- gram: float32 [4096, 4096], P('feat', ('node', 'tm'))
All inputs are finite; a program needn't handle non-finite values.
Results may differ from a plain program's by a relative error of at most 0.000073.
Values sent between devices are 32-bit elements; how exact they have to be, the bound alone decides.
No kernel may reach another device: no remote copies, remote signals or barrier semaphores. Data moves between devices by JAX's collectives and lax.ppermute only.
A program may use at most 128 MiB of HBM per device.

v0:
```python
import jax
import jax.numpy as jnp
from jax import lax
from jax.sharding import PartitionSpec as P


def body(tensor, basis):
    local_data = tensor[0]
    partial_proj = lax.dot_general(
        basis,
        local_data,
        (((0,), (0,)), ((), ())),
        precision=lax.Precision.HIGHEST,
        preferred_element_type=jnp.float32,
    )
    scale = 1.0 / (basis.shape[1] * lax.axis_size("tm"))
    block_proj = lax.psum(partial_proj, "node")
    full_proj = lax.all_gather(block_proj, "feat", axis=1, tiled=True)
    width = full_proj.shape[1] // lax.axis_size("node")
    columns = lax.dynamic_slice_in_dim(full_proj, lax.axis_index("node") * width, width, 1)
    term = lax.dot_general(
        block_proj,
        columns,
        (((0,), (0,)), ((), ())),
        precision=lax.Precision.HIGHEST,
        preferred_element_type=jnp.float32,
    )
    result = lax.psum_scatter(term * scale, "tm", scatter_dimension=1, tiled=True)
    return result


def solution(mesh):
    in_specs = (P("tm", "node", "feat"), P("node", None))
    out_specs = P("feat", ("node", "tm"))
    return jax.shard_map(body, mesh=mesh, in_specs=in_specs, out_specs=out_specs, check_vma=False)
```

profile of v0, /device:TPU:0, one launch (start us, length us, event | category | flops | bytes accessed | tf_op | source)
XLA Modules:
  0.0 141.4 jit_solution(4735564744402768312)
XLA Ops:
  6.5 0.0 copy-start
  6.5 0.0 all-reduce.2.cloned.1.call-start
  6.5 1.6 %copy-done = f32[4096,128]{1,0:T(8,128)S(1)} copy-done((f32[4096,128]{1,0:T(8,128)S(1)}, f32[4096,128]{1,0:T(8,128)}, u32[]{:S(2)}) %copy-start) | copy-done | bytes 2097176
  8.1 13.5 %fusion = f32[128,1024]{1,0:T(8,128)} fusion(f32[4096,128]{1,0:T(8,128)S(1)} %copy-done, f32[1,4096,1024]{2,1,0:T(8,128)} %param.2), kind=kOutput, calls=%fused_computation | convolution fusion | flops 6442450944 | bytes 19398656 | tf_op jit(solution)/shard_map/dot_general | solution.py:9
  21.6 0.0 all-reduce.2.cloned.1.call-update
  21.6 0.0 all-gather.2.cloned.1.call-start
  21.7 48.1 %all-reduce.2.cloned.1.call-done = f32[128,1024]{1,0:T(8,128)} async-done(((f32[128,1024]{1,0:T(8,128)}), f32[128,1024]{1,0:T(8,128)}) %all-reduce.2.cloned.1.call-update) | async-done | bytes 524304 | tf_op jit(solution)/shard_map/psum | solution.py:17
  69.8 0.0 all-gather.2.cloned.1.call-update
  69.8 0.0 reduce-scatter.2.cloned.1.call-start
  69.9 47.5 %all-gather.2.cloned.1.call-done = f32[128,4096]{1,0:T(8,128)} async-done(((f32[128,1024]{1,0:T(8,128)}), f32[128,4096]{1,0:T(8,128)}) %all-gather.2.cloned.1.call-update) | async-done | bytes 2097168 | tf_op jit(solution)/shard_map/all_gather | solution.py:18
  117.3 6.6 %convolution_multiply_fusion = f32[1024,1024]{1,0:T(8,128)} fusion(f32[128,1024]{1,0:T(8,128)} %all-reduce.2.cloned.1.call-done, f32[128,4096]{1,0:T(8,128)} %all-gather.2.cloned.1.call-done, s32[]{:T(128)S(6)} %select_n.3), kind=kOutput, calls=%fused_computation.2 | convolution fusion | flops 1611661312 | bytes 5242884 | tf_op jit(solution)/shard_map/dot_general | solution.py:21
  124.0 0.0 reduce-scatter.2.cloned.1.call-update
  124.0 10.9 %reduce-scatter.2.cloned.1.call-done = f32[1024,512]{1,0:T(8,128)} async-done(((f32[1024,1024]{1,0:T(8,128)}), f32[1024,512]{1,0:T(8,128)}) %reduce-scatter.2.cloned.1.call-update) | async-done | bytes 2097168 | tf_op jit(solution)/shard_map/reduce_scatter | solution.py:28
Async XLA Ops:
  6.5 1.6 %copy-start = (f32[4096,128]{1,0:T(8,128)S(1)}, f32[4096,128]{1,0:T(8,128)}, u32[]{:S(2)}) copy-start(f32[4096,128]{1,0:T(8,128)} %param.3) | copy-start | bytes 6291460
  6.5 63.3 %all-reduce.2.cloned.1.call-start = ((), (), s32[]{:S(2)}) async-start(), calls=%async_computation.1 | async-start | bytes 1048576 | tf_op jit(solution)/shard_map/psum | solution.py:17
  21.6 95.7 %all-gather.2.cloned.1.call-start = ((), (), s32[]{:S(2)}) async-start(), calls=%async_computation.2 | async-start | bytes 2621440 | tf_op jit(solution)/shard_map/all_gather | solution.py:18
  69.8 65.1 %reduce-scatter.2.cloned.1.call-start = ((), (), s32[]{:S(2)}) async-start(), calls=%async_computation.3 | async-start | bytes 6291456 | tf_op jit(solution)/shard_map/reduce_scatter | solution.py:28
Sparse Core Ops, SparseCore 0:
  21.7 48.0 all-reduce.1
  71.4 45.9 all-gather.1
  124.1 10.7 reduce-scatter.1
where the time goes:
time: 142 us; the launch traced here: 141 us
  waiting for transfers between devices  107 us (75%)
  matrix products  20.1 us (14%)
  between operations  13.1 us (9%)
  local copies, waits for them, and re-layouts  1.59 us (1%)
    psum x1, waiting for transfers between devices, body(): block_proj = lax.psum(partial_proj, 'node')  48.1 us
    all_gather x1, waiting for transfers between devices, body(): full_proj = lax.all_gather(block_proj, 'feat', axis=1, tiled=True)  47.5 us
    dot_general x1, matrix products, body(): lax.dot_general(basis, local_data, (((0,), (0,)), ((), ())), precision=la...  13.5 us
    reduce_scatter x1, waiting for transfers between devices, body(): lax.psum_scatter(term * scale, 'tm', scatter_dimension=1, tiled=True)  10.9 us
    dot_general x1, matrix products, body(): lax.dot_general(block_proj, columns, (((0,), (0,)), ((), ())), precision=...  6.61 us
  transfers between devices with their start and end apart: 3, of which 3 were waited for; matrix products, arithmetic and copies ran while one was open for 0% of the time, Pallas kernels for 0%

commit v1 on v0

--- a/solution.py
+++ b/solution.py
@@ -2,6 +2,23 @@
 import jax.numpy as jnp
 from jax import lax
 from jax.sharding import PartitionSpec as P
+
+
+def open_cycles(field_in, d0):
+    named_axis = "feat"
+    nd = lax.axis_size(named_axis)
+    chunks = [field_in]
+    for src_i in [*range(nd - 1)]:
+        chunks.append(
+            lax.ppermute(
+                chunks[-1],
+                axis_name=named_axis,
+                perm=[(tick, (tick + 1) % nd) for tick in range(nd)],
+            )
+        )
+    return jnp.roll(
+        jnp.concatenate(chunks[::-1], d0), (lax.axis_index(named_axis) + 1) * field_in.shape[d0], d0
+    )
 
 
 def body(tensor, basis):
@@ -15,7 +32,7 @@
     )
     scale = 1.0 / (basis.shape[1] * lax.axis_size("tm"))
     block_proj = lax.psum(partial_proj, "node")
-    full_proj = lax.all_gather(block_proj, "feat", axis=1, tiled=True)
+    full_proj = open_cycles(block_proj, d0=1)
     width = full_proj.shape[1] // lax.axis_size("node")
     columns = lax.dynamic_slice_in_dim(full_proj, lax.axis_index("node") * width, width, 1)
     term = lax.dot_general(

time: 142 us -> 141 us (level)
  waiting for transfers between devices: 107 us -> 99.8 us
  local copies, waits for them, and re-layouts: 1.59 us -> 7.09 us
  starting transfers between devices: 0.08 us -> 1.53 us
    all_gather x1 -> x0, waiting for transfers between devices: 47.5 us -> none  [body(): full_proj = lax.all_gather(block_proj, 'feat', axis=1, tiled=True)]
    ppermute x0 -> x3, waiting for transfers between devices: none -> 42.2 us  [open_cycles(): lax.ppermute(chunks[-1], axis_name=named_axis, perm=[(tick, (tick + 1) %...]
    unnamed x2 -> x11, local copies, waits for them, and re-layouts: 1.59 us -> 7.05 us
    reduce_scatter x1, waiting for transfers between devices: 10.9 us -> 9.4 us  [body(): lax.psum_scatter(term * scale, 'tm', scatter_dimension=1, tiled=True)]
    ppermute x0 -> x3, starting transfers between devices: none -> 1.49 us  [open_cycles(): lax.ppermute(chunks[-1], axis_name=named_axis, perm=[(tick, (tick + 1) %...]
  transfers between devices with their start and end apart: 3 -> 5, of which waited for: 3 -> 5; matrix products, arithmetic and copies ran while one was open for 0% -> 0% of each run, Pallas kernels for 0% -> 0%
where the time goes in v1:
time: 141 us
  waiting for transfers between devices  99.8 us (71%)
  matrix products  18.7 us (13%)
  between operations  13.5 us (10%)
  local copies, waits for them, and re-layouts  7.09 us (5%)
  starting transfers between devices  1.53 us (1%)
    psum x1, waiting for transfers between devices, body(): block_proj = lax.psum(partial_proj, 'node')  48.1 us
    ppermute x3, waiting for transfers between devices, open_cycles(): lax.ppermute(chunks[-1], axis_name=named_axis, perm=[(tick, (tick + 1) %...  42.2 us
    dot_general x1, matrix products, body(): lax.dot_general(basis, local_data, (((0,), (0,)), ((), ())), precision=la...  13.5 us
    reduce_scatter x1, waiting for transfers between devices, body(): lax.psum_scatter(term * scale, 'tm', scatter_dimension=1, tiled=True)  9.4 us
    unnamed x11, local copies, waits for them, and re-layouts  7.05 us
    dot_general x1, matrix products, body(): lax.dot_general(block_proj, columns, (((0,), (0,)), ((), ())), precision=...  5.24 us
  transfers between devices with their start and end apart: 5, of which 5 were waited for; matrix products, arithmetic and copies ran while one was open for 0% of the time, Pallas kernels for 0%

profile of v1, /device:TPU:0, one launch (start us, length us, event | category | flops | bytes accessed | tf_op | source)
XLA Modules:
  0.0 140.6 jit_solution(5207033099549631223)
XLA Ops:
  6.5 0.0 copy-start
  6.5 0.0 all-reduce.2.cloned.1.call-start
  6.5 1.6 %copy-done = f32[4096,128]{1,0:T(8,128)S(1)} copy-done((f32[4096,128]{1,0:T(8,128)S(1)}, f32[4096,128]{1,0:T(8,128)}, u32[]{:S(2)}) %copy-start) | copy-done | bytes 2097176
  8.1 13.5 %fusion = f32[128,1024]{1,0:T(8,128)} fusion(f32[4096,128]{1,0:T(8,128)S(1)} %copy-done, f32[1,4096,1024]{2,1,0:T(8,128)} %param.2), kind=kOutput, calls=%fused_computation | convolution fusion | flops 6442450944 | bytes 19398656 | tf_op jit(solution)/shard_map/dot_general | solution.py:26
  21.6 0.0 all-reduce.2.cloned.1.call-update
  21.6 0.0 reduce-scatter.2.cloned.1.call-start
  21.7 48.1 %all-reduce.2.cloned.1.call-done = f32[128,1024]{1,0:T(8,128)} async-done(((f32[128,1024]{1,0:T(8,128)}), f32[128,1024]{1,0:T(8,128)}) %all-reduce.2.cloned.1.call-update) | async-done | bytes 524304 | tf_op jit(solution)/shard_map/psum | solution.py:34
  69.8 0.0 copy-start.1
  69.8 1.5 %collective-permute-start = (f32[128,1024]{1,0:T(8,128)}, f32[128,1024]{1,0:T(8,128)S(1)}, u32[]{:S(2)}, u32[]{:S(2)}) collective-permute-start(f32[128,1024]{1,0:T(8,128)} %all-reduce.2.cloned.1.call-done), channel_id=1, source_target_pairs={{0,2},{2,4},{4,6},{6,0},{1,3},{3,5},{5,7},{7,1},{8,10},{10,12},{12... | collective-permute-start | bytes 1572872 | tf_op jit(solution)/shard_map/ppermute | solution.py:13
  71.3 14.0 %collective-permute-done = f32[128,1024]{1,0:T(8,128)S(1)} collective-permute-done((f32[128,1024]{1,0:T(8,128)}, f32[128,1024]{1,0:T(8,128)S(1)}, u32[]{:S(2)}, u32[]{:S(2)}) %collective-permute-start) | collective-permute-done | bytes 524320 | tf_op jit(solution)/shard_map/ppermute | solution.py:13
  85.3 0.0 collective-permute-start.1
  85.3 14.5 %collective-permute-done.1 = f32[128,1024]{1,0:T(8,128)} collective-permute-done((f32[128,1024]{1,0:T(8,128)S(1)}, f32[128,1024]{1,0:T(8,128)}, u32[]{:S(2)}, u32[]{:S(2)}) %collective-permute-start.1) | collective-permute-done | bytes 524320 | tf_op jit(solution)/shard_map/ppermute | solution.py:13
  99.8 0.0 collective-permute-start.2
  99.8 13.8 %collective-permute-done.2 = f32[128,1024]{1,0:T(8,128)} collective-permute-done((f32[128,1024]{1,0:T(8,128)}, f32[128,1024]{1,0:T(8,128)}, u32[]{:S(2)}, u32[]{:S(2)}) %collective-permute-start.2) | collective-permute-done | bytes 524320 | tf_op jit(solution)/shard_map/ppermute | solution.py:13
  113.6 1.1 constant_dynamic-update-slice_fusion.7
  114.6 1.1 constant_dynamic-update-slice_fusion.6
  115.8 1.1 constant_dynamic-update-slice_fusion.4
  116.9 1.1 constant_dynamic-update-slice_fusion.3
  117.9 1.1 constant_dynamic-update-slice_fusion.2
  119.1 0.0 copy-done.1
  119.1 5.2 %convolution_multiply_fusion = f32[1024,1024]{1,0:T(8,128)} fusion(f32[128,1024]{1,0:T(8,128)S(1)} %copy-done.1, f32[128,8192]{1,0:T(8,128)S(1)} %constant_dynamic-update-slice_fusion, s32[]{:T(128)S(6)} %dynamic_slice.8), kind=kOutput, calls=%fused_computation.2 | convolution fusion | flops 1611661312 | bytes 5242884 | tf_op jit(solution)/shard_map/dot_general | solution.py:38
  124.4 0.0 reduce-scatter.2.cloned.1.call-update
  124.4 9.4 %reduce-scatter.2.cloned.1.call-done = f32[1024,512]{1,0:T(8,128)} async-done(((f32[1024,1024]{1,0:T(8,128)}), f32[1024,512]{1,0:T(8,128)}) %reduce-scatter.2.cloned.1.call-update) | async-done | bytes 2097168 | tf_op jit(solution)/shard_map/reduce_scatter | solution.py:45
  (3 shorter events, 0.1 us)
Async XLA Ops:
  6.5 1.6 %copy-start = (f32[4096,128]{1,0:T(8,128)S(1)}, f32[4096,128]{1,0:T(8,128)}, u32[]{:S(2)}) copy-start(f32[4096,128]{1,0:T(8,128)} %param.3) | copy-start | bytes 6291460
  6.5 63.3 %all-reduce.2.cloned.1.call-start = ((), (), s32[]{:S(2)}) async-start(), calls=%async_computation.1 | async-start | bytes 1048576 | tf_op jit(solution)/shard_map/psum | solution.py:34
  21.6 112.2 %reduce-scatter.2.cloned.1.call-start = ((), (), s32[]{:S(2)}) async-start(), calls=%async_computation.2 | async-start | bytes 6291456 | tf_op jit(solution)/shard_map/reduce_scatter | solution.py:45
  69.8 49.3 %copy-start.1 = (f32[128,1024]{1,0:T(8,128)S(1)}, f32[128,1024]{1,0:T(8,128)}, u32[]{:S(2)}) copy-start(f32[128,1024]{1,0:T(8,128)} %all-reduce.2.cloned.1.call-done) | copy-start | bytes 1572868
  69.8 15.5 %collective-permute-start = (f32[128,1024]{1,0:T(8,128)}, f32[128,1024]{1,0:T(8,128)S(1)}, u32[]{:S(2)}, u32[]{:S(2)}) collective-permute-start(f32[128,1024]{1,0:T(8,128)} %all-reduce.2.cloned.1.call-done), channel_id=1, source_target_pairs={{0,2},{2,4},{4,6},{6,0},{1,3},{3,5},{5,7},{7,1},{8,10},{10,12},{12... | collective-permute-start | bytes 1572872 | tf_op jit(solution)/shard_map/ppermute | solution.py:13
  85.3 14.5 %collective-permute-start.1 = (f32[128,1024]{1,0:T(8,128)S(1)}, f32[128,1024]{1,0:T(8,128)}, u32[]{:S(2)}, u32[]{:S(2)}) collective-permute-start(f32[128,1024]{1,0:T(8,128)S(1)} %collective-permute-done), channel_id=1, source_target_pairs={{0,2},{2,4},{4,6},{6,0},{1,3},{3,5},{5,7},{7,1},{8,10},{10,12},{12... | collective-permute-start | bytes 1572872 | tf_op jit(solution)/shard_map/ppermute | solution.py:13
  99.8 13.8 %collective-permute-start.2 = (f32[128,1024]{1,0:T(8,128)}, f32[128,1024]{1,0:T(8,128)}, u32[]{:S(2)}, u32[]{:S(2)}) collective-permute-start(f32[128,1024]{1,0:T(8,128)} %collective-permute-done.1), channel_id=1, source_target_pairs={{0,2},{2,4},{4,6},{6,0},{1,3},{3,5},{5,7},{7,1},{8,10},{10,12},{12... | collective-permute-start | bytes 1572872 | tf_op jit(solution)/shard_map/ppermute | solution.py:13
Sparse Core Ops, SparseCore 0:
  21.7 48.0 all-reduce.1
  124.5 9.2 reduce-scatter.1

commit v2 on v0

--- a/solution.py
+++ b/solution.py
@@ -2,6 +2,11 @@
 import jax.numpy as jnp
 from jax import lax
 from jax.sharding import PartitionSpec as P
+
+
+def summed_here(x, name):
+    parts = lax.all_gather(x, name)
+    return jnp.sum(parts, axis=0)
 
 
 def body(tensor, basis):
@@ -14,7 +19,7 @@
         preferred_element_type=jnp.float32,
     )
     scale = 1.0 / (basis.shape[1] * lax.axis_size("tm"))
-    block_proj = lax.psum(partial_proj, "node")
+    block_proj = summed_here(partial_proj, "node")
     full_proj = lax.all_gather(block_proj, "feat", axis=1, tiled=True)
     width = full_proj.shape[1] // lax.axis_size("node")
     columns = lax.dynamic_slice_in_dim(full_proj, lax.axis_index("node") * width, width, 1)

time: 142 us -> 133 us (0.937)
  waiting for transfers between devices: 107 us -> 95.1 us
  other arithmetic: 0 us -> 2.59 us
    psum x1 -> x0, waiting for transfers between devices: 48.1 us -> none  [body(): block_proj = lax.psum(partial_proj, 'node')]
    all_gather x0 -> x1, waiting for transfers between devices: none -> 38.1 us  [summed_here(): parts = lax.all_gather(x, name)]
    reduce_sum x0 -> x1, other arithmetic: none -> 2.59 us  [summed_here(): return jnp.sum(parts, axis=0)]
    all_gather x1, waiting for transfers between devices: 47.5 us -> 46 us  [body(): full_proj = lax.all_gather(block_proj, 'feat', axis=1, tiled=True)]
where the time goes in v2:
time: 133 us
  waiting for transfers between devices  95.1 us (72%)
  matrix products  20.1 us (15%)
  between operations  13.1 us (10%)
  other arithmetic  2.59 us (2%)
  local copies, waits for them, and re-layouts  1.59 us (1%)
    all_gather x1, waiting for transfers between devices, body(): full_proj = lax.all_gather(block_proj, 'feat', axis=1, tiled=True)  46 us
    all_gather x1, waiting for transfers between devices, summed_here(): parts = lax.all_gather(x, name)  38.1 us
    dot_general x1, matrix products, body(): lax.dot_general(basis, local_data, (((0,), (0,)), ((), ())), precision=la...  13.5 us
    reduce_scatter x1, waiting for transfers between devices, body(): lax.psum_scatter(term * scale, 'tm', scatter_dimension=1, tiled=True)  10.9 us
    dot_general x1, matrix products, body(): lax.dot_general(block_proj, columns, (((0,), (0,)), ((), ())), precision=...  6.61 us
  transfers between devices with their start and end apart: 3, of which 3 were waited for; matrix products, arithmetic and copies ran while one was open for 0% of the time, Pallas kernels for 0%

profile of v2, /device:TPU:0, one launch (start us, length us, event | category | flops | bytes accessed | tf_op | source)
XLA Modules:
  0.0 132.6 jit_solution(9680432985759834078)
XLA Ops:
  6.5 0.0 copy-start
  6.5 0.0 all-gather.6.cloned.1.call-start
  6.5 1.6 %copy-done = f32[4096,128]{1,0:T(8,128)S(1)} copy-done((f32[4096,128]{1,0:T(8,128)S(1)}, f32[4096,128]{1,0:T(8,128)}, u32[]{:S(2)}) %copy-start) | copy-done | bytes 2097176
  8.1 13.5 %fusion = f32[128,1024]{1,0:T(8,128)} fusion(f32[4096,128]{1,0:T(8,128)S(1)} %copy-done, f32[1,4096,1024]{2,1,0:T(8,128)} %param.2), kind=kOutput, calls=%fused_computation | convolution fusion | flops 6442450944 | bytes 19398656 | tf_op jit(solution)/shard_map/dot_general | solution.py:14
  21.6 0.0 all-gather.6.cloned.1.call-update
  21.6 0.0 all-gather.4.cloned.1.call-start
  21.7 38.1 %all-gather.6.cloned.1.call-done = f32[512,1024]{1,0:T(8,128)} async-done(((f32[128,1024]{1,0:T(8,128)}), f32[512,1024]{1,0:T(8,128)}) %all-gather.6.cloned.1.call-update) | async-done | bytes 2097168 | tf_op jit(solution)/shard_map/all_gather | solution.py:8
  59.8 2.6 %reduce_sum.9 = f32[128,1024]{1,0:T(8,128)} reduce(f32[4,128,1024]{2,1,0:T(8,128)} %bitcast.6, f32[]{:T(128)} %constant.6.clone.1), dimensions={0}, to_apply=%region_0.0 | reduce | flops 393216 | bytes 2621444 | tf_op jit(solution)/shard_map/reduce_sum | solution.py:9
  62.4 0.0 all-gather.4.cloned.1.call-update
  62.4 0.0 reduce-scatter.2.cloned.1.call-start
  62.5 46.0 %all-gather.4.cloned.1.call-done = f32[128,4096]{1,0:T(8,128)} async-done(((f32[128,1024]{1,0:T(8,128)}), f32[128,4096]{1,0:T(8,128)}) %all-gather.4.cloned.1.call-update) | async-done | bytes 2097168 | tf_op jit(solution)/shard_map/all_gather | solution.py:23
  108.5 6.6 %convolution_multiply_fusion = f32[1024,1024]{1,0:T(8,128)} fusion(f32[128,1024]{1,0:T(8,128)} %reduce_sum.9, f32[128,4096]{1,0:T(8,128)} %all-gather.4.cloned.1.call-done, s32[]{:T(128)S(6)} %select_n.3), kind=kOutput, calls=%fused_computation.2 | convolution fusion | flops 1611661312 | bytes 5242884 | tf_op jit(solution)/shard_map/dot_general | solution.py:26
  115.1 0.0 reduce-scatter.2.cloned.1.call-update
  115.1 10.9 %reduce-scatter.2.cloned.1.call-done = f32[1024,512]{1,0:T(8,128)} async-done(((f32[1024,1024]{1,0:T(8,128)}), f32[1024,512]{1,0:T(8,128)}) %reduce-scatter.2.cloned.1.call-update) | async-done | bytes 2097168 | tf_op jit(solution)/shard_map/reduce_scatter | solution.py:33
Async XLA Ops:
  6.5 1.6 %copy-start = (f32[4096,128]{1,0:T(8,128)S(1)}, f32[4096,128]{1,0:T(8,128)}, u32[]{:S(2)}) copy-start(f32[4096,128]{1,0:T(8,128)} %param.3) | copy-start | bytes 6291460
  6.5 53.2 %all-gather.6.cloned.1.call-start = ((), (), s32[]{:S(2)}) async-start(), calls=%async_computation.3 | async-start | bytes 2621440 | tf_op jit(solution)/shard_map/all_gather | solution.py:8
  21.6 86.9 %all-gather.4.cloned.1.call-start = ((), (), s32[]{:S(2)}) async-start(), calls=%async_computation.1 | async-start | bytes 2621440 | tf_op jit(solution)/shard_map/all_gather | solution.py:23
  62.4 63.6 %reduce-scatter.2.cloned.1.call-start = ((), (), s32[]{:S(2)}) async-start(), calls=%async_computation.2 | async-start | bytes 6291456 | tf_op jit(solution)/shard_map/reduce_scatter | solution.py:33
Sparse Core Ops, SparseCore 0:
  21.7 38.0 all-gather.5
  62.5 45.9 all-gather.3
  115.2 10.7 reduce-scatter.1
